TPU v7x, 32 devices: a whole 2x2x4 slice. The times are simulated.
32 devices in a mesh: island: 4 (over z), fsdp: 2 (over x), tensor: 4 (over y, core).
Axes of the slice: x: 2, y: 2, z: 4, core: 2. Of those that a mesh axis runs over, the one named last changes fastest.
Arguments:
- hidden: bfloat16 [4, 256, 14336], P('island', 'fsdp', 'tensor'), may hold values from -6 to 6
- target: bfloat16 [4, 256, 4096], P('island', 'tensor', 'fsdp'), may hold values from -6 to 6
- valid: int32 [4, 256], P('island', 'fsdp'), may hold values from 0 to 1, as said below
- island_tokens: int32 [4], replicated, may hold values from 4096 to 16384
- inner_weight: bfloat16 [4, 14336, 4096], P('island', 'tensor', 'fsdp'), may hold values from -6 to 6
- adam_first: bfloat16 [4, 14336, 4096], P('island', 'tensor', 'fsdp'), may hold values from -0.0014648438 to 0.0014648438
- adam_second: bfloat16 [4, 14336, 4096], P('island', 'tensor', 'fsdp'), may hold values from 6.798655e-08 to 1.0877848e-06
- anchor: bfloat16 [14336, 4096], P('tensor', 'fsdp'), may hold values from -6 to 6
- outer_momentum: bfloat16 [14336, 4096], P('tensor', 'fsdp'), may hold values from -6 to 6
Outputs:
- new_weight: bfloat16 [14336, 4096], P('tensor', 'fsdp')
- new_momentum: bfloat16 [14336, 4096], P('tensor', 'fsdp')
Inputs may be any that keep to these rules, and one draw needn't show every extreme that they name: The first token of each block of 128 tokens is valid.
All inputs are finite; a program needn't handle non-finite values.
Results may differ from a plain program's by a relative error of at most 0.003.
Values may be sent and summed in bfloat16 or wider, within the bound.
No kernel may reach another device: no remote copies, remote signals or barrier semaphores. Data moves between devices by JAX's collectives and lax.ppermute only.
A program may use at most 320 MiB of HBM per device.

v0:
```python
import jax
import jax.numpy as jnp
from jax import lax
from jax.sharding import PartitionSpec as P

FFW = 14336
beta_first = 0.9
beta_second = 0.95
epsilon = 1e-08
inner_rate = 0.5
decay_rate = 0.1
outer_rate = 0.7
nesterov_mu = 0.9


def nesterov(anchor_part, moment_part, average_step):
    momentum = nesterov_mu * moment_part.astype(jnp.float32) + average_step
    updated = anchor_part.astype(jnp.float32) - outer_rate * (average_step + nesterov_mu * momentum)
    return (updated.astype(jnp.bfloat16), momentum.astype(jnp.bfloat16))


def on_device(
    hidden,
    target,
    valid,
    island_tokens,
    inner_weight,
    adam_first,
    adam_second,
    anchor,
    outer_momentum,
):
    factor = FFW ** (-0.5)
    keep_mask = valid[0].astype(jnp.bfloat16)
    masked = hidden[0] * keep_mask[:, None]
    tallies = lax.psum(jnp.sum(valid[0].astype(jnp.float32)), "fsdp")
    gathered = lax.all_gather(masked, "fsdp", axis=0, tiled=True)
    partial_out = factor * jnp.dot(gathered, inner_weight[0], preferred_element_type=jnp.float32)
    full_target = lax.all_gather(target[0], "tensor", axis=0, tiled=True)
    summed = lax.psum(partial_out.astype(jnp.bfloat16), "tensor").astype(jnp.float32)
    cotangent = ((summed - full_target.astype(jnp.float32)) / tallies).astype(jnp.bfloat16)
    gradient = factor * lax.dot_general(
        gathered, cotangent, (((0,), (0,)), ((), ())), preferred_element_type=jnp.float32
    )
    weights = inner_weight[0].astype(jnp.float32)
    first = beta_first * adam_first[0].astype(jnp.float32) + (1.0 - beta_first) * gradient
    second = (
        beta_second * adam_second[0].astype(jnp.float32) + (1.0 - beta_second) * gradient * gradient
    )
    inner_new = weights - inner_rate * (first / (jnp.sqrt(second) + epsilon) + decay_rate * weights)
    totals = island_tokens.astype(jnp.float32)
    portion = totals[lax.axis_index("island")] / jnp.sum(totals)
    weighted = portion * (anchor.astype(jnp.float32) - inner_new)
    average_step = lax.psum(weighted, "island")
    return nesterov(anchor, outer_momentum, average_step)


def solution(mesh):
    return jax.shard_map(
        on_device,
        mesh=mesh,
        in_specs=(
            P("island", "fsdp", "tensor"),
            P("island", "tensor", "fsdp"),
            P("island", "fsdp"),
            P(),
            P("island", "tensor", "fsdp"),
            P("island", "tensor", "fsdp"),
            P("island", "tensor", "fsdp"),
            P("tensor", "fsdp"),
            P("tensor", "fsdp"),
        ),
        out_specs=(P("tensor", "fsdp"), P("tensor", "fsdp")),
        check_vma=False,
    )
```

profile of v0, /device:TPU:0, one launch (start us, length us, event | category | flops | bytes accessed | tf_op | source)
XLA Modules:
  0.0 1147.3 jit_solution(17382033286298603500)
XLA Ops:
  7.2 0.0 copy-start.1
  7.2 0.0 copy-start.2
  7.2 0.0 all-gather.4.cloned.1.call-start
  7.2 0.7 convert_bitcast_fusion
  7.9 2.2 bitcast_multiply_fusion
  10.1 0.0 all-gather.4.cloned.1.call-update
  10.2 0.0 all-gather.6.cloned.1.call-start
  10.2 0.7 all-gather.6.cloned.1.call-update
  10.9 0.0 all-reduce.3.cloned.1.call-start
  11.0 32.2 %all-gather.4.cloned.1.call-done = bf16[256,3584]{1,0:T(8,128)(2,1)} async-done(((bf16[128,3584]{1,0:T(8,128)(2,1)}), bf16[256,3584]{1,0:T(8,128)(2,1)}) %all-gather.4.cloned.1.call-update) | async-done | bytes 1835024 | tf_op jit(solution)/shard_map/all_gather | solution.py:37
  43.2 0.0 copy-start
  43.2 10.8 fusion.13
  54.0 0.0 all-reduce.3.cloned.1.call-update
  54.0 0.0 all-reduce.5.cloned.1.call-start
  54.0 0.0 copy-done.1
  54.0 0.6 convert_reduce_fusion
  54.7 5.8 psum.22
  60.5 0.0 copy-done.2
  60.5 0.6 dynamic_slice.3
  61.1 0.7 convert_reduce_fusion.1
  63.1 0.0 all-gather.6.cloned.1.call-done
  63.1 37.4 %all-reduce.3.cloned.1.call-done = bf16[256,2048]{1,0:T(8,128)(2,1)} async-done(((bf16[256,2048]{1,0:T(8,128)(2,1)}), bf16[256,2048]{1,0:T(8,128)(2,1)}) %all-reduce.3.cloned.1.call-update) | async-done | bytes 1048592 | tf_op jit(solution)/shard_map/psum | solution.py:40
  100.6 0.0 copy-done
  100.6 40.1 %fusion = f32[3584,2048]{1,0:T(8,128)} fusion(bf16[3584,2048]{1,0:T(8,128)(2,1)} %param.16, bf16[1,3584,2048]{2,1,0:T(8,128)(2,1)} %param.15, bf16[1,3584,2048]{2,1,0:T(8,128)(2,1)} %param.14, bf16[1,3584,2048]{2,1,0:T(8,128)(2,1)} %param.13, f32[]{:T(128)S(6)} %div.12, bf16[256,3584]{1,0:T(8,128)(2,1)S(1)} %copy-done, ...), kind=kOutput, calls=%fused_computation.4 | convolution fusion | flops 3907518464 | bytes 92012552 | tf_op jit(solution)/shard_map/dot_general | solution.py:42
  140.6 0.0 all-reduce.5.cloned.1.call-update
  140.7 968.3 %all-reduce.5.cloned.1.call-done = f32[3584,2048]{1,0:T(8,128)} async-done(((f32[3584,2048]{1,0:T(8,128)}), f32[3584,2048]{1,0:T(8,128)}) %all-reduce.5.cloned.1.call-update) | async-done | bytes 29360144 | tf_op jit(solution)/shard_map/psum | solution.py:54
  1108.9 31.9 %fusion.7 = (bf16[3584,2048]{1,0:T(8,128)(2,1)}, bf16[3584,2048]{1,0:T(8,128)(2,1)}) fusion(f32[3584,2048]{1,0:T(8,128)} %all-reduce.5.cloned.1.call-done, bf16[3584,2048]{1,0:T(8,128)(2,1)} %param.17, bf16[3584,2048]{1,0:T(8,128)(2,1)} %param.16), kind=kLoop, calls=%fused_computation.14 | loop fusion | flops 73400320 | bytes 88080384 | tf_op jit(solution)/shard_map/convert_element_type | solution.py:19
  (1 shorter events, 0.0 us)
Async XLA Ops:
  7.2 46.9 %copy-start.1 = (s32[1,128]{1,0:T(1,128)S(1)}, s32[1,128]{1,0:T(1,128)}, u32[]{:S(2)}) copy-start(s32[1,128]{1,0:T(1,128)} %param.11) | copy-start | bytes 1540
  7.2 53.3 %copy-start.2 = (s32[4]{0:T(128)S(1)}, s32[4]{0:T(128)}, u32[]{:S(2)}) copy-start(s32[4]{0:T(128)} %param.12) | copy-start | bytes 52
  7.2 36.0 %all-gather.4.cloned.1.call-start = ((), (), s32[]{:S(2)}) async-start(), calls=%async_computation | async-start | bytes 2752512 | tf_op jit(solution)/shard_map/all_gather | solution.py:37
  10.2 53.0 %all-gather.6.cloned.1.call-start = ((), (), s32[]{:S(2)}) async-start(), calls=%async_computation.3 | async-start | bytes 1310720 | tf_op jit(solution)/shard_map/all_gather | solution.py:39
  10.9 89.6 %all-reduce.3.cloned.1.call-start = ((), (), s32[]{:S(2)}) async-start(), calls=%async_computation.1 | async-start | bytes 2097152 | tf_op jit(solution)/shard_map/psum | solution.py:40
  43.2 57.4 %copy-start = (bf16[256,3584]{1,0:T(8,128)(2,1)S(1)}, bf16[256,3584]{1,0:T(8,128)(2,1)}, u32[]{:S(2)}) copy-start(bf16[256,3584]{1,0:T(8,128)(2,1)} %all-gather.4.cloned.1.call-done) | copy-start | bytes 5505028
  54.0 1054.9 %all-reduce.5.cloned.1.call-start = ((), (), s32[]{:S(2)}) async-start(), calls=%async_computation.2 | async-start | bytes 58720256 | tf_op jit(solution)/shard_map/psum | solution.py:54
Sparse Core Ops, SparseCore 0:
  10.3 32.8 all-gather.3
  44.7 16.7 all-gather.5
  64.4 36.0 all-reduce.2
  140.8 968.0 all-reduce.4
where the time goes:
time: 1150 us
  waiting for transfers between devices  1040 us (90%)
  matrix products  50.9 us (4%)
  other arithmetic  36 us (3%)
  between operations  15.2 us (1%)
    psum x1, waiting for transfers between devices, on_device(): average_step = lax.psum(weighted, 'island')  968 us
    dot_general x1, matrix products, on_device(): lax.dot_general(gathered, cotangent, (((0,), (0,)), ((), ())), preferred_...  40.1 us
    psum x1, waiting for transfers between devices, on_device(): lax.psum(partial_out.astype(jnp.bfloat16), 'tensor').astype(jnp.float32)  37.4 us
    all_gather x1, waiting for transfers between devices, on_device(): gathered = lax.all_gather(masked, 'fsdp', axis=0, tiled=True)  32.2 us
    convert_element_type x1, other arithmetic, nesterov(): return (updated.astype(jnp.bfloat16), momentum.astype(jnp.bfloat16))  31.9 us
  transfers between devices with their start and end apart: 4, of which 3 were waited for; matrix products, arithmetic and copies ran while one was open for 1% of the time, Pallas kernels for 0%

commit v1 on v0

--- a/solution.py
+++ b/solution.py
@@ -51,7 +51,7 @@
     totals = island_tokens.astype(jnp.float32)
     portion = totals[lax.axis_index("island")] / jnp.sum(totals)
     weighted = portion * (anchor.astype(jnp.float32) - inner_new)
-    average_step = lax.psum(weighted, "island")
+    average_step = jnp.sum(lax.all_gather(weighted, "island"), axis=0)
     return nesterov(anchor, outer_momentum, average_step)
 
 

time: 1150 us -> 2160 us (1.88)
  waiting for transfers between devices: 1040 us -> 2010 us
  other arithmetic: 36 us -> 83.2 us
    all_gather x0 -> x1, waiting for transfers between devices: none -> 1940 us  [on_device(): average_step = jnp.sum(lax.all_gather(weighted, 'island'), axis=0)]
    psum x1 -> x0, waiting for transfers between devices: 968 us -> none  [on_device(): average_step = lax.psum(weighted, 'island')]
    reduce_sum x0 -> x1, other arithmetic: none -> 47.2 us  [on_device(): average_step = jnp.sum(lax.all_gather(weighted, 'island'), axis=0)]
where the time goes in v1:
time: 2160 us
  waiting for transfers between devices  2010 us (93%)
  other arithmetic  83.2 us (4%)
  matrix products  51.1 us (2%)
    all_gather x1, waiting for transfers between devices, on_device(): average_step = jnp.sum(lax.all_gather(weighted, 'island'), axis=0)  1940 us
    reduce_sum x1, other arithmetic, on_device(): average_step = jnp.sum(lax.all_gather(weighted, 'island'), axis=0)  47.2 us
  transfers between devices with their start and end apart: 4, of which 3 were waited for; matrix products, arithmetic and copies ran while one was open for 1% of the time, Pallas kernels for 0%

profile of v1, /device:TPU:0, one launch (start us, length us, event | category | flops | bytes accessed | tf_op | source)
XLA Modules:
  0.0 2161.5 jit_solution(16520393599806580842)
XLA Ops:
  7.2 0.0 copy-start.1
  7.2 0.0 copy-start.2
  7.2 0.0 all-gather.6.cloned.1.call-start
  7.2 0.7 convert_bitcast_fusion
  7.9 2.2 bitcast_multiply_fusion
  10.1 0.0 all-gather.6.cloned.1.call-update
  10.2 0.0 all-gather.8.cloned.1.call-start
  10.2 0.7 all-gather.8.cloned.1.call-update
  10.9 0.0 all-reduce.2.cloned.1.call-start
  11.0 32.2 %all-gather.6.cloned.1.call-done = bf16[256,3584]{1,0:T(8,128)(2,1)} async-done(((bf16[128,3584]{1,0:T(8,128)(2,1)}), bf16[256,3584]{1,0:T(8,128)(2,1)}) %all-gather.6.cloned.1.call-update) | async-done | bytes 1835024 | tf_op jit(solution)/shard_map/all_gather | solution.py:37
  43.2 0.0 copy-start
  43.2 10.8 fusion.13
  54.0 0.0 all-reduce.2.cloned.1.call-update
  54.0 0.0 all-gather.10.cloned.1.call-start
  54.0 0.0 copy-done.1
  54.0 0.6 convert_reduce_fusion
  54.6 5.8 psum.15
  60.4 0.0 copy-done.2
  60.4 0.6 dynamic_slice.3
  61.0 0.6 convert_reduce_fusion.1
  62.9 0.0 all-gather.8.cloned.1.call-done
  63.0 37.7 %all-reduce.2.cloned.1.call-done = bf16[256,2048]{1,0:T(8,128)(2,1)} async-done(((bf16[256,2048]{1,0:T(8,128)(2,1)}), bf16[256,2048]{1,0:T(8,128)(2,1)}) %all-reduce.2.cloned.1.call-update) | async-done | bytes 1048592 | tf_op jit(solution)/shard_map/psum | solution.py:40
  100.6 0.0 copy-done
  100.6 40.3 %fusion = f32[3584,2048]{1,0:T(8,128)} fusion(bf16[3584,2048]{1,0:T(8,128)(2,1)} %param.16, bf16[1,3584,2048]{2,1,0:T(8,128)(2,1)} %param.15, bf16[1,3584,2048]{2,1,0:T(8,128)(2,1)} %param.14, bf16[1,3584,2048]{2,1,0:T(8,128)(2,1)} %param.13, f32[]{:T(128)S(6)} %div.12, bf16[256,3584]{1,0:T(8,128)(2,1)S(1)} %copy-done, ...), kind=kOutput, calls=%fused_computation.4 | convolution fusion | flops 3907518464 | bytes 92012552 | tf_op jit(solution)/shard_map/dot_general | solution.py:42
  140.9 0.0 all-gather.10.cloned.1.call-update
  140.9 1935.0 %all-gather.10.cloned.1.call-done = f32[14336,2048]{1,0:T(8,128)} async-done(((f32[3584,2048]{1,0:T(8,128)}), f32[14336,2048]{1,0:T(8,128)}) %all-gather.10.cloned.1.call-update) | async-done | bytes 117440528 | tf_op jit(solution)/shard_map/all_gather | solution.py:54
  2075.9 47.2 %reduce_sum.29 = f32[3584,2048]{1,0:T(8,128)} reduce(f32[4,3584,2048]{2,1,0:T(8,128)} %bitcast.7, f32[]{:T(128)} %constant.6.clone.1), dimensions={0}, to_apply=%region_4.0 | reduce | flops 22020096 | bytes 146800640 | tf_op jit(solution)/shard_map/reduce_sum | solution.py:54
  2123.1 31.9 %fusion.7 = (bf16[3584,2048]{1,0:T(8,128)(2,1)}, bf16[3584,2048]{1,0:T(8,128)(2,1)}) fusion(f32[3584,2048]{1,0:T(8,128)} %reduce_sum.29, bf16[3584,2048]{1,0:T(8,128)(2,1)} %param.17, bf16[3584,2048]{1,0:T(8,128)(2,1)} %param.16), kind=kLoop, calls=%fused_computation.14 | loop fusion | flops 73400320 | bytes 88080384 | tf_op jit(solution)/shard_map/convert_element_type | solution.py:19
  (1 shorter events, 0.0 us)
Async XLA Ops:
  7.2 46.9 %copy-start.1 = (s32[1,128]{1,0:T(1,128)S(1)}, s32[1,128]{1,0:T(1,128)}, u32[]{:S(2)}) copy-start(s32[1,128]{1,0:T(1,128)} %param.11) | copy-start | bytes 1540
  7.2 53.2 %copy-start.2 = (s32[4]{0:T(128)S(1)}, s32[4]{0:T(128)}, u32[]{:S(2)}) copy-start(s32[4]{0:T(128)} %param.12) | copy-start | bytes 52
  7.2 36.0 %all-gather.6.cloned.1.call-start = ((), (), s32[]{:S(2)}) async-start(), calls=%async_computation | async-start | bytes 2752512 | tf_op jit(solution)/shard_map/all_gather | solution.py:37
  10.2 52.8 %all-gather.8.cloned.1.call-start = ((), (), s32[]{:S(2)}) async-start(), calls=%async_computation.2 | async-start | bytes 1310720 | tf_op jit(solution)/shard_map/all_gather | solution.py:39
  10.9 89.7 %all-reduce.2.cloned.1.call-start = ((), (), s32[]{:S(2)}) async-start(), calls=%async_computation.1 | async-start | bytes 2097152 | tf_op jit(solution)/shard_map/psum | solution.py:40
  43.2 57.4 %copy-start = (bf16[256,3584]{1,0:T(8,128)(2,1)S(1)}, bf16[256,3584]{1,0:T(8,128)(2,1)}, u32[]{:S(2)}) copy-start(bf16[256,3584]{1,0:T(8,128)(2,1)} %all-gather.6.cloned.1.call-done) | copy-start | bytes 5505028
  54.0 2021.9 %all-gather.10.cloned.1.call-start = ((), (), s32[]{:S(2)}) async-start(), calls=%async_computation.3 | async-start | bytes 146800640 | tf_op jit(solution)/shard_map/all_gather | solution.py:54
Sparse Core Ops, SparseCore 0:
  10.3 32.8 all-gather.5
  44.7 16.7 all-gather.7
  64.4 36.1 all-reduce.1
  141.0 1934.8 all-gather.9
